TPU v7x, 512 devices: a whole 4x8x8 slice. The times are simulated.
512 devices in a mesh: row: 32 (over y_lo, x, core), col: 16 (over z, y_hi).
Axes of the slice: x: 4, y: 8 (y_hi: 2, y_lo: 4; y = y_hi * 4 + y_lo), z: 8, core: 2. Of those that a mesh axis runs over, the one named last changes fastest.
Arguments:
- telemetry: int32 [65536, 64], P(('col', 'row')), may hold values from -127 to 127
- scales: int32 [65536], P(('col', 'row')), may hold values from 1 to 4
- bands: int32 [32, 32], replicated, may hold values from 256 to 4096
- noise: float32 [65536], P('row'), may hold values from 0.5 to 2
- start: bfloat16 [65536, 64], P(('col', 'row')), may hold values from -6 to 6
- target: bfloat16 [65536, 64], P('row'), may hold values from -6 to 6
Outputs:
- first: float32 [65536, 64], P('row')
- second: float32 [65536, 64], P('row')
All inputs are finite; a program needn't handle non-finite values.
Results may differ from a plain program's by a relative error of at most 0.0023.
Values may be sent and summed in bfloat16 or wider, within the bound.
A program may use at most 128 MiB of HBM per device.

v0:
```python
import math
import jax
import jax.numpy as jnp
from jax import lax
from jax.sharding import Mesh
from jax.sharding import PartitionSpec as P

SUBAP = 2048
COL = ("col_0", "col_1")
COL_ROW = ("col_0", "col_1", "row")
damping = 0.4


def laid_out(parts, dim):
    parts = jnp.moveaxis(parts, 0, dim)
    dims = parts.shape
    return parts.reshape(*dims[:dim], dims[dim] * dims[dim + 1], *dims[dim + 2 :])


def copy_for_each(array, axis):
    copies = jnp.broadcast_to(array, (lax.axis_size(axis), *array.shape))
    return lax.all_to_all(copies, axis, split_axis=0, concat_axis=0, tiled=True)


def collect(array, axis, dim):
    return laid_out(copy_for_each(array, axis), dim)


def broadcast_by_axis(array, axes, root):
    array = jnp.where(lax.axis_index(axes) == root, array, jnp.zeros_like(array))
    for axis in axes:
        array = lax.psum(array, axis)
    return array


def split_up(array, dim, count):
    dims = array.shape
    parts = array.reshape(*dims[:dim], count, dims[dim] // count, *dims[dim + 1 :])
    return jnp.moveaxis(parts, dim, 0)


def sent_and_summed(array, axis, dim):
    count = lax.axis_size(axis)
    parts = lax.all_to_all(split_up(array, dim, count), axis, 0, 0, tiled=True)
    return jnp.sum(parts, axis=0)


def broadcast(array, axis, root):
    return lax.dynamic_index_in_dim(lax.all_gather(array, axis), root, 0, keepdims=False)


def on_device(telemetry, scales, bands, noise, start, target):
    frame_count = telemetry.shape[1]
    row_count = lax.axis_size("row")
    col_count = lax.axis_size(COL)
    ratio = row_count // col_count
    row_id = lax.axis_index("row")
    col_id = lax.axis_index(COL)
    order_total = telemetry.shape[0] * row_count * col_count
    norm_count = jnp.float32(order_total // 4)
    slopes = (telemetry.astype(jnp.float32) * scales.astype(jnp.float32)[:, None] / 128.0).astype(
        jnp.bfloat16
    )
    joined = jnp.concatenate([slopes, start], axis=1)
    col_joined = collect(joined, "row", 0)
    col_width = col_joined.shape[0]
    row_height = col_width // ratio
    half = lax.dynamic_slice_in_dim(col_joined, row_id % ratio * row_height, row_height, 0)
    row_joined = broadcast_by_axis(half, COL, row_id // ratio)
    row_slopes = row_joined[:, :frame_count]
    row_start = row_joined[:, frame_count:]
    col_slopes = col_joined[:, :frame_count]
    col_start = col_joined[:, frame_count:]
    panel_width = col_start.shape[1]
    row_f = row_slopes.astype(jnp.float32)
    weight = damping / (jnp.sum(row_f * row_f, axis=1) / norm_count + noise)
    count = bands.shape[0]
    index = jnp.arange(count, dtype=jnp.int32)
    sym = jnp.where(index[:, None] <= index[None, :], bands, bands.T).astype(jnp.float32)
    row_ids = row_id * row_height + jnp.arange(row_height, dtype=jnp.int32)
    onehot = (row_ids[:, None] // SUBAP == index[None, :]).astype(jnp.float32)
    row_band = jnp.dot(onehot, sym, precision=lax.Precision.HIGHEST)
    row_pos = (row_ids % SUBAP).astype(jnp.float32)
    width = math.gcd(math.gcd(col_width, 512), SUBAP)
    nblocks = col_width // width

    def build(step, carry):
        tile, acc = carry
        offset = step * width
        cols = lax.dynamic_slice_in_dim(col_slopes, offset, width, 0)
        raw = (
            lax.dot_general(
                row_slopes, cols, (((1,), (1,)), ((), ())), preferred_element_type=jnp.float32
            )
            / norm_count
        )
        col_ids = col_id * col_width + offset + jnp.arange(width, dtype=jnp.int32)
        band = lax.dynamic_slice_in_dim(row_band, (col_id * col_width + offset) // SUBAP, 1, 1)
        dist = jnp.abs(row_pos[:, None] - (col_ids % SUBAP).astype(jnp.float32)[None, :])
        taper = jnp.maximum(0.0, 1.0 - dist / band)
        diag = jnp.where(row_ids[:, None] == col_ids[None, :], noise[:, None], jnp.float32(0.0))
        entry = (taper * raw + diag).astype(jnp.bfloat16)
        tile = lax.dynamic_update_slice_in_dim(tile, entry, offset, 1)
        return (tile, acc)

    tile_init = jnp.zeros((row_height, col_width), jnp.bfloat16)
    acc_init = jnp.zeros((row_height, panel_width), jnp.float32)
    tile, acc = lax.fori_loop(0, nblocks, build, (tile_init, acc_init))
    product0 = jnp.dot(tile, col_start, preferred_element_type=jnp.float32)
    target_f = target.astype(jnp.float32)

    def refine(current, product):
        share = sent_and_summed(product, COL, 0)
        share_rows = row_height // col_count
        begin = col_id * share_rows
        cur_part = lax.dynamic_slice_in_dim(current, begin, share_rows, 0)
        tgt_part = lax.dynamic_slice_in_dim(target_f, begin, share_rows, 0)
        wgt_part = lax.dynamic_slice_in_dim(weight, begin, share_rows, 0)
        updated = cur_part + wgt_part[:, None] * (tgt_part - share)
        return collect(updated, COL, 0)

    first = refine(row_start.astype(jnp.float32), product0)
    first_low = first.astype(jnp.bfloat16)
    pieces = [broadcast(first_low, "row", col_id * ratio + offset_q) for offset_q in range(ratio)]
    col_first = jnp.concatenate(pieces, axis=0)
    product1 = jnp.dot(tile, col_first, preferred_element_type=jnp.float32)
    second = refine(first, product1)
    return (first, second)


def solution(mesh):
    finer = Mesh(mesh.devices.reshape(mesh.shape["row"], 8, 2), ("row", "col_0", "col_1"))
    placed = (P(COL_ROW, None), P(COL_ROW), P(), P("row"), P(COL_ROW, None), P("row", None))
    return jax.shard_map(
        on_device,
        mesh=finer,
        in_specs=placed,
        out_specs=(P("row", None), P("row", None)),
        check_vma=False,
    )
```

profile of v0, /device:TPU:10, one launch (start us, length us, event | category | flops | bytes accessed | tf_op | source)
XLA Modules:
  0.0 425.8 jit_solution(2020574549629206897)
XLA Ops:
  9.3 1.2 broadcast_in_dim.58
  10.5 9.5 %all-to-all-start = ((bf16[32,128,128]{1,2,0:T(8,128)(2,1)}), bf16[32,128,128]{1,2,0:T(8,128)(2,1)S(1)}, u32[]{:S(2)}, u32[]{:S(2)}) async-start(bf16[32,128,128]{1,2,0:T(8,128)(2,1)} %broadcast_in_dim.58), calls=%async_computation | async-start | bytes 2097152 | tf_op jit(solution)/shard_map/all_to_all | solution.py:22
  20.1 24.6 %all-to-all-done = bf16[32,128,128]{1,2,0:T(8,128)(2,1)S(1)} async-done(((bf16[32,128,128]{1,2,0:T(8,128)(2,1)}), bf16[32,128,128]{1,2,0:T(8,128)(2,1)S(1)}, u32[]{:S(2)}, u32[]{:S(2)}) %all-to-all-start) | async-done | bytes 1048608 | tf_op jit(solution)/shard_map/all_to_all | solution.py:22
  46.6 81.7 %all-reduce.3.cloned.1.call-done = bf16[2048,128]{0,1:T(8,128)(2,1)} async-done(((bf16[2048,128]{0,1:T(8,128)(2,1)}), bf16[2048,128]{0,1:T(8,128)(2,1)}) %all-reduce.3.cloned.1.call-update) | async-done | bytes 524304 | tf_op jit(solution)/shard_map/psum | solution.py:32
  129.3 59.7 %all-reduce.5.cloned.1.call-done = bf16[2048,128]{0,1:T(8,128)(2,1)} async-done(((bf16[2048,128]{0,1:T(8,128)(2,1)}), bf16[2048,128]{0,1:T(8,128)(2,1)}) %all-reduce.5.cloned.1.call-update) | async-done | bytes 524304 | tf_op jit(solution)/shard_map/psum | solution.py:32
  190.3 6.0 %broadcast_in_dim.60 = bf16[2048,4096]{0,1:T(8,128)(2,1)} broadcast(bf16[]{:T(256)} %constant.210.clone.1), dimensions={} | broadcast | bytes 16777218 | tf_op jit(solution)/shard_map/broadcast_in_dim | solution.py:106
  196.3 23.1 %while.17 = (s32[]{:T(128)}, bf16[2048,4096]{0,1:T(8,128)(2,1)}, s32[]{:T(128)}, f32[2048,32]{0,1:T(8,128)S(1)}, bf16[4096,64]{1,0:T(8,128)(2,1)S(1)}, /*index=5...) while((s32[]{:T(128)}, bf16[2048,4096]{0,1:T(8,128)(2,1)}, ...), condition=%wide.region_4.5_spmd.clone.clone, body=%wide.region_3.4_spmd.clone.clone.sunk | while | flops 145785376 | bytes 2827667 | solution.py:108
  196.4 2.9 fusion.45
  199.3 2.8 fusion.45
  202.2 2.8 fusion.45
  205.1 2.9 fusion.45
  208.0 2.8 fusion.45
  210.9 2.8 fusion.45
  213.8 2.8 fusion.45
  216.7 2.8 fusion.45
  219.5 9.0 %convolution_bitcast_fusion.1 = f32[8,16,8,128]{3,2,1,0:T(8,128)S(1)} fusion(bf16[2048,4096]{0,1:T(8,128)(2,1)} %get-tuple-element.227, bf16[4096,128]{1,0:T(8,128)(2,1)S(1)} %bitcast.53), kind=kOutput, calls=%fused_computation.22 | convolution fusion | flops 1073741824 | bytes 18350080 | tf_op jit(solution)/shard_map/dot_general | solution.py:109
  229.3 8.3 %all-to-all-start.1 = ((f32[16,128,64]{1,2,0:T(8,128)}), f32[16,128,64]{1,2,0:T(8,128)S(1)}, u32[]{:S(2)}, u32[]{:S(2)}) async-start(f32[16,128,64]{1,2,0:T(8,128)} %bitcast.43), calls=%async_computation.1 | async-start | bytes 1048576 | tf_op jit(solution)/shard_map/all_to_all | solution.py:44
  237.8 20.3 %all-to-all-done.1 = f32[16,128,64]{1,2,0:T(8,128)S(1)} async-done(((f32[16,128,64]{1,2,0:T(8,128)}), f32[16,128,64]{1,2,0:T(8,128)S(1)}, u32[]{:S(2)}, u32[]{:S(2)}) %all-to-all-start.1) | async-done | bytes 524320 | tf_op jit(solution)/shard_map/all_to_all | solution.py:44
  258.9 24.4 %all_to_all.25 = f32[16,128,64]{1,2,0:T(8,128)S(1)} all-to-all(f32[16,128,64]{1,2,0:T(8,128)S(1)} %broadcast_in_dim.61), channel_id=1, replica_groups=mesh['row'=32,'col_0'=8,'col_1'=2] {'col_0','col_1'}, dimensions={0} | all-to-all | bytes 1048576 | tf_op jit(solution)/shard_map/all_to_all | solution.py:22
  284.4 65.9 %all-gather.2.cloned.1.call-done = bf16[32,2048,64]{1,2,0:T(8,128)(2,1)} async-done(((bf16[1,2048,64]{1,2,0:T(8,128)(2,1)}), bf16[32,2048,64]{1,2,0:T(8,128)(2,1)}) %all-gather.2.cloned.1.call-update) | async-done | bytes 8388624 | tf_op jit(solution)/shard_map/all_gather | solution.py:49
  351.3 8.8 %convolution_bitcast_fusion = f32[8,16,8,128]{3,2,1,0:T(8,128)S(1)} fusion(bf16[2048,4096]{0,1:T(8,128)(2,1)} %get-tuple-element.227, bf16[2048,64]{0,1:T(8,128)(2,1)S(1)} %get-tuple-element.325, bf16[2048,64]{0,1:T(8,128)(2,1)S(1)} %get-tuple-element.324), kind=kOutput, calls=%fused_computation.21 | convolution fusion | flops 1074790400 | bytes 17825792 | tf_op jit(solution)/shard_map/dot_general | solution.py:126
  361.0 11.1 %all-to-all-start.3 = ((f32[16,128,64]{1,2,0:T(8,128)}), f32[16,128,64]{1,2,0:T(8,128)S(1)}, u32[]{:S(2)}, u32[]{:S(2)}) async-start(f32[16,128,64]{1,2,0:T(8,128)} %bitcast.42), calls=%async_computation.3 | async-start | bytes 1048576 | tf_op jit(solution)/shard_map/all_to_all | solution.py:44
  372.1 21.0 %all-to-all-done.3 = f32[16,128,64]{1,2,0:T(8,128)S(1)} async-done(((f32[16,128,64]{1,2,0:T(8,128)}), f32[16,128,64]{1,2,0:T(8,128)S(1)}, u32[]{:S(2)}, u32[]{:S(2)}) %all-to-all-start.3) | async-done | bytes 524320 | tf_op jit(solution)/shard_map/all_to_all | solution.py:44
  394.0 24.5 %all_to_all.26 = f32[16,128,64]{1,2,0:T(8,128)S(1)} all-to-all(f32[16,128,64]{1,2,0:T(8,128)S(1)} %broadcast_in_dim.62), channel_id=1, replica_groups=mesh['row'=32,'col_0'=8,'col_1'=2] {'col_0','col_1'}, dimensions={0} | all-to-all | bytes 1048576 | tf_op jit(solution)/shard_map/all_to_all | solution.py:22
  (66 shorter events, 13.1 us)
Async XLA Ops:
  10.5 117.8 %copy-start.2 = (s32[32,32]{1,0:T(8,128)S(1)}, s32[32,32]{1,0:T(8,128)}, u32[]{:S(2)}) copy-start(s32[32,32]{1,0:T(8,128)} %param.10) | copy-start | bytes 12292
  10.5 34.2 %all-to-all-start = ((bf16[32,128,128]{1,2,0:T(8,128)(2,1)}), bf16[32,128,128]{1,2,0:T(8,128)(2,1)S(1)}, u32[]{:S(2)}, u32[]{:S(2)}) async-start(bf16[32,128,128]{1,2,0:T(8,128)(2,1)} %broadcast_in_dim.58), calls=%async_computation | async-start | bytes 2097152 | tf_op jit(solution)/shard_map/all_to_all | solution.py:22
  20.1 108.2 %all-reduce.3.cloned.1.call-start = ((), (), s32[]{:S(2)}) async-start(), calls=%async_computation.5 | async-start | bytes 1048576 | tf_op jit(solution)/shard_map/psum | solution.py:32
  46.5 142.4 %all-reduce.5.cloned.1.call-start = ((), (), s32[]{:S(2)}) async-start(), calls=%async_computation.6 | async-start | bytes 1048576 | tf_op jit(solution)/shard_map/psum | solution.py:32
  190.3 6.0 %copy-start.3 = (f32[2048]{0:T(1024)S(1)}, f32[2048]{0:T(1024)}, u32[]{:S(2)}) copy-start(f32[2048]{0:T(1024)} %param.11) | copy-start | bytes 24580
  219.5 18.2 %copy-start = (bf16[2048,128]{0,1:T(8,128)(2,1)S(1)}, bf16[2048,128]{0,1:T(8,128)(2,1)}, u32[]{:S(2)}) copy-start(bf16[2048,128]{0,1:T(8,128)(2,1)} %all-reduce.5.cloned.1.call-done) | copy-start | bytes 1572868
  229.3 28.8 %all-to-all-start.1 = ((f32[16,128,64]{1,2,0:T(8,128)}), f32[16,128,64]{1,2,0:T(8,128)S(1)}, u32[]{:S(2)}, u32[]{:S(2)}) async-start(f32[16,128,64]{1,2,0:T(8,128)} %bitcast.43), calls=%async_computation.1 | async-start | bytes 1048576 | tf_op jit(solution)/shard_map/all_to_all | solution.py:44
  237.6 112.7 %all-gather.2.cloned.1.call-start = ((), (), s32[]{:S(2)}) async-start(), calls=%async_computation.7 | async-start | bytes 8650752 | tf_op jit(solution)/shard_map/all_gather | solution.py:49
  361.0 32.2 %all-to-all-start.3 = ((f32[16,128,64]{1,2,0:T(8,128)}), f32[16,128,64]{1,2,0:T(8,128)S(1)}, u32[]{:S(2)}, u32[]{:S(2)}) async-start(f32[16,128,64]{1,2,0:T(8,128)} %bitcast.42), calls=%async_computation.3 | async-start | bytes 1048576 | tf_op jit(solution)/shard_map/all_to_all | solution.py:44
  372.1 47.2 %copy-start.1 = (f32[2048,64]{0,1:T(8,128)}, f32[2048,64]{0,1:T(8,128)S(1)}, u32[]{:S(2)}) copy-start(f32[2048,64]{0,1:T(8,128)S(1)} %copy_bitcast_fusion.1) | copy-start | bytes 1572868
Sparse Core Ops, SparseCore 0:
  46.7 81.5 all-reduce.2
  131.2 57.7 all-reduce.4
  284.5 65.7 all-gather.1
where the time goes:
time: 427 us; the launch traced here: 426 us
  waiting for transfers between devices  273 us (64%)
  blocking collectives  48.8 us (11%)
  matrix products  41.3 us (10%)
  starting transfers between devices  29 us (7%)
  local copies, waits for them, and re-layouts  14.4 us (3%)
  between operations  14 us (3%)
  other arithmetic  4.94 us (1%)
    psum x2, waiting for transfers between devices, broadcast_by_axis(): array = lax.psum(array, axis)  141 us
    all_gather x1, waiting for transfers between devices, broadcast(): lax.all_gather(array, axis)  65.9 us
    all_to_all x2, blocking collectives, copy_for_each(): return lax.all_to_all(copies, axis, split_axis=0, concat_axis=0, tiled=True)  48.8 us
    all_to_all x2, waiting for transfers between devices, sent_and_summed(): parts = lax.all_to_all(split_up(array, dim, count), axis, 0, 0, tiled=True)  41.3 us
    all_to_all x1, waiting for transfers between devices, copy_for_each(): return lax.all_to_all(copies, axis, split_axis=0, concat_axis=0, tiled=True)  24.6 us
    dot_general x8, matrix products, build(): lax.dot_general(row_slopes, cols, (((1,), (1,)), ((), ())), preferred_ele...  22.7 us
    all_to_all x2, starting transfers between devices, sent_and_summed(): parts = lax.all_to_all(split_up(array, dim, count), axis, 0, 0, tiled=True)  19.3 us
    all_to_all x1, starting transfers between devices, copy_for_each(): return lax.all_to_all(copies, axis, split_axis=0, concat_axis=0, tiled=True)  9.54 us
  transfers between devices with their start and end apart: 6, of which 6 were waited for; matrix products, arithmetic and copies ran while one was open for 0% of the time, Pallas kernels for 0%

commit v1 on v0

--- a/solution.py
+++ b/solution.py
@@ -29,7 +29,7 @@
 def broadcast_by_axis(array, axes, root):
     array = jnp.where(lax.axis_index(axes) == root, array, jnp.zeros_like(array))
     for axis in axes:
-        array = lax.psum(array, axis)
+        array = jnp.sum(lax.all_gather(array, axis), axis=0)
     return array
 
 

time: 427 us -> 388 us (0.909)
  waiting for transfers between devices: 273 us -> 231 us
  other arithmetic: 4.94 us -> 10.7 us
    psum x2 -> x0, waiting for transfers between devices: 141 us -> none  [broadcast_by_axis(): array = lax.psum(array, axis)]
    all_gather x0 -> x2, waiting for transfers between devices: none -> 101 us  [broadcast_by_axis(): array = jnp.sum(lax.all_gather(array, axis), axis=0)]
    reduce_sum x0 -> x2, other arithmetic: none -> 5.4 us  [broadcast_by_axis(): array = jnp.sum(lax.all_gather(array, axis), axis=0)]
where the time goes in v1:
time: 388 us; the launch traced here: 387 us
  waiting for transfers between devices  231 us (60%)
  blocking collectives  49 us (13%)
  matrix products  41.2 us (11%)
  starting transfers between devices  29 us (7%)
  between operations  14 us (4%)
  local copies, waits for them, and re-layouts  12.5 us (3%)
  other arithmetic  10.7 us (3%)
    all_gather x2, waiting for transfers between devices, broadcast_by_axis(): array = jnp.sum(lax.all_gather(array, axis), axis=0)  101 us
    all_gather x1, waiting for transfers between devices, broadcast(): lax.all_gather(array, axis)  65.8 us
    all_to_all x2, blocking collectives, copy_for_each(): return lax.all_to_all(copies, axis, split_axis=0, concat_axis=0, tiled=True)  49 us
    all_to_all x2, waiting for transfers between devices, sent_and_summed(): parts = lax.all_to_all(split_up(array, dim, count), axis, 0, 0, tiled=True)  39.5 us
    all_to_all x1, waiting for transfers between devices, copy_for_each(): return lax.all_to_all(copies, axis, split_axis=0, concat_axis=0, tiled=True)  24.6 us
    dot_general x8, matrix products, build(): lax.dot_general(row_slopes, cols, (((1,), (1,)), ((), ())), preferred_ele...  22.7 us
    all_to_all x2, starting transfers between devices, sent_and_summed(): parts = lax.all_to_all(split_up(array, dim, count), axis, 0, 0, tiled=True)  19.4 us
    all_to_all x1, starting transfers between devices, copy_for_each(): return lax.all_to_all(copies, axis, split_axis=0, concat_axis=0, tiled=True)  9.54 us
  transfers between devices with their start and end apart: 6, of which 6 were waited for; matrix products, arithmetic and copies ran while one was open for 0% of the time, Pallas kernels for 0%

profile of v1, /device:TPU:10, one launch (start us, length us, event | category | flops | bytes accessed | tf_op | source)
XLA Modules:
  0.0 387.3 jit_solution(12561691702450836523)
XLA Ops:
  10.6 9.5 %all-to-all-start = ((bf16[32,128,128]{2,1,0:T(8,128)(2,1)}), bf16[32,128,128]{2,1,0:T(8,128)(2,1)S(1)}, u32[]{:S(2)}, u32[]{:S(2)}) async-start(bf16[32,128,128]{2,1,0:T(8,128)(2,1)} %broadcast_in_dim.58), calls=%async_computation | async-start | bytes 2097152 | tf_op jit(solution)/shard_map/all_to_all | solution.py:22
  20.3 24.6 %all-to-all-done = bf16[32,128,128]{2,1,0:T(8,128)(2,1)S(1)} async-done(((bf16[32,128,128]{2,1,0:T(8,128)(2,1)}), bf16[32,128,128]{2,1,0:T(8,128)(2,1)S(1)}, u32[]{:S(2)}, u32[]{:S(2)}) %all-to-all-start) | async-done | bytes 1048608 | tf_op jit(solution)/shard_map/all_to_all | solution.py:22
  45.9 59.9 %all-gather.8.cloned.1.call-done = bf16[16384,128]{1,0:T(8,128)(2,1)} async-done(((bf16[2048,128]{1,0:T(8,128)(2,1)}), bf16[16384,128]{1,0:T(8,128)(2,1)}) %all-gather.8.cloned.1.call-update) | async-done | bytes 4194320 | tf_op jit(solution)/shard_map/all_gather | solution.py:32
  105.8 3.7 reduce_sum.51
  110.5 40.8 %all-gather.10.cloned.1.call-done = bf16[4096,128]{1,0:T(8,128)(2,1)} async-done(((bf16[2048,128]{1,0:T(8,128)(2,1)}), bf16[4096,128]{1,0:T(8,128)(2,1)}) %all-gather.10.cloned.1.call-update) | async-done | bytes 1048592 | tf_op jit(solution)/shard_map/all_gather | solution.py:32
  153.2 6.0 %broadcast_in_dim.60 = bf16[2048,4096]{0,1:T(8,128)(2,1)} broadcast(bf16[]{:T(256)} %constant.212.clone.1), dimensions={} | broadcast | bytes 16777218 | tf_op jit(solution)/shard_map/broadcast_in_dim | solution.py:106
  159.2 23.1 %while.17 = (s32[]{:T(128)}, bf16[2048,4096]{0,1:T(8,128)(2,1)}, s32[]{:T(128)}, f32[2048,32]{0,1:T(8,128)S(1)}, bf16[4096,64]{1,0:T(8,128)(2,1)S(1)}, /*index=5...) while((s32[]{:T(128)}, bf16[2048,4096]{0,1:T(8,128)(2,1)}, ...), condition=%wide.region_4.5_spmd.clone.clone, body=%wide.region_3.4_spmd.clone.clone.sunk | while | flops 145785376 | bytes 2827667 | solution.py:108
  159.2 2.9 fusion.45
  162.1 2.8 fusion.45
  165.0 2.8 fusion.45
  167.9 2.8 fusion.45
  170.8 2.8 fusion.45
  173.7 2.8 fusion.45
  176.6 2.8 fusion.45
  179.5 2.8 fusion.45
  182.3 8.9 %convolution_bitcast_fusion.1 = f32[8,16,8,128]{3,2,1,0:T(8,128)S(1)} fusion(bf16[2048,4096]{0,1:T(8,128)(2,1)} %get-tuple-element.227, bf16[4096,128]{1,0:T(8,128)(2,1)S(1)} %bitcast.55), kind=kOutput, calls=%fused_computation.22 | convolution fusion | flops 1073741824 | bytes 18350080 | tf_op jit(solution)/shard_map/dot_general | solution.py:109
  192.0 8.3 %all-to-all-start.1 = ((f32[16,128,64]{1,2,0:T(8,128)}), f32[16,128,64]{1,2,0:T(8,128)S(1)}, u32[]{:S(2)}, u32[]{:S(2)}) async-start(f32[16,128,64]{1,2,0:T(8,128)} %bitcast.45), calls=%async_computation.1 | async-start | bytes 1048576 | tf_op jit(solution)/shard_map/all_to_all | solution.py:44
  201.0 18.5 %all-to-all-done.1 = f32[16,128,64]{1,2,0:T(8,128)S(1)} async-done(((f32[16,128,64]{1,2,0:T(8,128)}), f32[16,128,64]{1,2,0:T(8,128)S(1)}, u32[]{:S(2)}, u32[]{:S(2)}) %all-to-all-start.1) | async-done | bytes 524320 | tf_op jit(solution)/shard_map/all_to_all | solution.py:44
  220.3 24.4 %all_to_all.25 = f32[16,128,64]{1,2,0:T(8,128)S(1)} all-to-all(f32[16,128,64]{1,2,0:T(8,128)S(1)} %broadcast_in_dim.61), channel_id=1, replica_groups=mesh['row'=32,'col_0'=8,'col_1'=2] {'col_0','col_1'}, dimensions={0} | all-to-all | bytes 1048576 | tf_op jit(solution)/shard_map/all_to_all | solution.py:22
  245.8 65.8 %all-gather.6.cloned.1.call-done = bf16[32,2048,64]{1,2,0:T(8,128)(2,1)} async-done(((bf16[1,2048,64]{1,2,0:T(8,128)(2,1)}), bf16[32,2048,64]{1,2,0:T(8,128)(2,1)}) %all-gather.6.cloned.1.call-update) | async-done | bytes 8388624 | tf_op jit(solution)/shard_map/all_gather | solution.py:49
  312.7 8.8 %convolution_bitcast_fusion = f32[8,16,8,128]{3,2,1,0:T(8,128)S(1)} fusion(bf16[2048,4096]{0,1:T(8,128)(2,1)} %get-tuple-element.227, bf16[2048,64]{0,1:T(8,128)(2,1)S(1)} %get-tuple-element.325, bf16[2048,64]{0,1:T(8,128)(2,1)S(1)} %get-tuple-element.324), kind=kOutput, calls=%fused_computation.21 | convolution fusion | flops 1074790400 | bytes 17825792 | tf_op jit(solution)/shard_map/dot_general | solution.py:126
  322.3 11.1 %all-to-all-start.3 = ((f32[16,128,64]{1,2,0:T(8,128)}), f32[16,128,64]{1,2,0:T(8,128)S(1)}, u32[]{:S(2)}, u32[]{:S(2)}) async-start(f32[16,128,64]{1,2,0:T(8,128)} %bitcast.44), calls=%async_computation.3 | async-start | bytes 1048576 | tf_op jit(solution)/shard_map/all_to_all | solution.py:44
  333.5 21.1 %all-to-all-done.3 = f32[16,128,64]{1,2,0:T(8,128)S(1)} async-done(((f32[16,128,64]{1,2,0:T(8,128)}), f32[16,128,64]{1,2,0:T(8,128)S(1)}, u32[]{:S(2)}, u32[]{:S(2)}) %all-to-all-start.3) | async-done | bytes 524320 | tf_op jit(solution)/shard_map/all_to_all | solution.py:44
  355.3 24.6 %all_to_all.26 = f32[16,128,64]{1,2,0:T(8,128)S(1)} all-to-all(f32[16,128,64]{1,2,0:T(8,128)S(1)} %broadcast_in_dim.62), channel_id=1, replica_groups=mesh['row'=32,'col_0'=8,'col_1'=2] {'col_0','col_1'}, dimensions={0} | all-to-all | bytes 1048576 | tf_op jit(solution)/shard_map/all_to_all | solution.py:22
  (65 shorter events, 14.5 us)
Async XLA Ops:
  10.6 98.9 %copy-start.1 = (s32[32,32]{1,0:T(8,128)S(1)}, s32[32,32]{1,0:T(8,128)}, u32[]{:S(2)}) copy-start(s32[32,32]{1,0:T(8,128)} %param.10) | copy-start | bytes 12292
  10.6 34.2 %all-to-all-start = ((bf16[32,128,128]{2,1,0:T(8,128)(2,1)}), bf16[32,128,128]{2,1,0:T(8,128)(2,1)S(1)}, u32[]{:S(2)}, u32[]{:S(2)}) async-start(bf16[32,128,128]{2,1,0:T(8,128)(2,1)} %broadcast_in_dim.58), calls=%async_computation | async-start | bytes 2097152 | tf_op jit(solution)/shard_map/all_to_all | solution.py:22
  20.2 85.6 %all-gather.8.cloned.1.call-start = ((), (), s32[]{:S(2)}) async-start(), calls=%async_computation.6 | async-start | bytes 4718592 | tf_op jit(solution)/shard_map/all_gather | solution.py:32
  45.8 105.4 %all-gather.10.cloned.1.call-start = ((), (), s32[]{:S(2)}) async-start(), calls=%async_computation.7 | async-start | bytes 1572864 | tf_op jit(solution)/shard_map/all_gather | solution.py:32
  153.1 6.0 %copy-start.2 = (f32[2048]{0:T(1024)S(1)}, f32[2048]{0:T(1024)}, u32[]{:S(2)}) copy-start(f32[2048]{0:T(1024)} %param.11) | copy-start | bytes 24580
  192.0 27.4 %all-to-all-start.1 = ((f32[16,128,64]{1,2,0:T(8,128)}), f32[16,128,64]{1,2,0:T(8,128)S(1)}, u32[]{:S(2)}, u32[]{:S(2)}) async-start(f32[16,128,64]{1,2,0:T(8,128)} %bitcast.45), calls=%async_computation.1 | async-start | bytes 1048576 | tf_op jit(solution)/shard_map/all_to_all | solution.py:44
  200.4 111.2 %all-gather.6.cloned.1.call-start = ((), (), s32[]{:S(2)}) async-start(), calls=%async_computation.5 | async-start | bytes 8650752 | tf_op jit(solution)/shard_map/all_gather | solution.py:49
  322.3 32.2 %all-to-all-start.3 = ((f32[16,128,64]{1,2,0:T(8,128)}), f32[16,128,64]{1,2,0:T(8,128)S(1)}, u32[]{:S(2)}, u32[]{:S(2)}) async-start(f32[16,128,64]{1,2,0:T(8,128)} %bitcast.44), calls=%async_computation.3 | async-start | bytes 1048576 | tf_op jit(solution)/shard_map/all_to_all | solution.py:44
  333.4 47.3 %copy-start = (f32[2048,64]{0,1:T(8,128)}, f32[2048,64]{0,1:T(8,128)S(1)}, u32[]{:S(2)}) copy-start(f32[2048,64]{0,1:T(8,128)S(1)} %copy_bitcast_fusion.1) | copy-start | bytes 1572868
Sparse Core Ops, SparseCore 0:
  45.9 59.8 all-gather.7
  109.6 41.5 all-gather.9
  245.9 65.6 all-gather.5
